TPU v7x, 32 devices: a whole 2x2x4 slice. The times are simulated.
32 devices in a mesh: groups: 2 (over y), sect: 16 (over z, x, core).
Axes of the slice: x: 2, y: 2, z: 4, core: 2. Of those that a mesh axis runs over, the one named last changes fastest.
Arguments:
- pattern: int32 [32], P('sect'), may hold values from 0 to 15
- thickness: float32 [32], P('sect'), may hold values from 0.5 to 1.5
- coupling: float32 [16, 2, 169, 169], replicated, may hold values from -0.0625 to 0.0625
- angles: float32 [64, 169], replicated, may hold values from -3.140625 to 3.140625
- points: int32 [2], P('groups'), parts along dimension 0, may hold values from 0 to 63
- incident: float32 [2, 2, 169, 169], P('groups'), parts along dimension 0, may hold values from -6 to 6
- monitors: int32 [16], replicated, may hold values from 0 to 168
- weights: float32 [16], replicated, may hold values from 0.05 to 0.5
Outputs:
- fields: float32 [32, 2, 2, 169, 169], P('sect', 'groups'), parts along dimension 1
- gradient: float32 [2, 32], P('groups', 'sect'), parts along dimension 0
There are 2 independent parts, one for each index of `groups`. A program takes and returns all parts, laid end to end along the dimension named above; an argument that names none is the same for every part. Nothing has to cross between parts.
All inputs are finite; a program needn't handle non-finite values.
Results may differ from a plain program's by a relative error of at most 0.0003.
Values sent between devices are 32-bit elements; how exact they have to be, the bound alone decides.
A program may use at most 128 MiB of HBM per device.

v0:
```python
import jax
import jax.numpy as jnp
from jax import lax
from jax.sharding import PartitionSpec as P

norm_scale = (1.0 + 1.0 / 22.0) ** (-0.5)
highest = lax.Precision.HIGHEST


def entering(shard, axis, combine, identity, reverse):
    length, here = (lax.axis_size(axis), lax.axis_index(axis))
    everything = jax.tree.map(lambda part: lax.all_gather(part, axis), shard)
    start = jax.tree.map(
        lambda part, zero: jnp.broadcast_to(jnp.asarray(zero, part.dtype), part.shape),
        shard,
        identity,
    )

    def hop(k, before):
        at = length - 1 - k if reverse else k
        reached = at > here if reverse else at < here
        new = combine(before, jax.tree.map(lambda part: part[at], everything))
        return jax.tree.map(lambda a, b: jnp.where(reached, a, b), new, before)

    return lax.fori_loop(0, length, hop, start)


def spread(block, axis, source):
    block = jnp.where(lax.axis_index(axis) == source, block, jnp.zeros_like(block))
    return lax.psum(block, axis)


def complex_product(left, right):
    left_real, left_imag = left
    right_real, right_imag = right
    out_real = jnp.einsum("pij,pjk->pik", left_real, right_real, precision=highest) - jnp.einsum(
        "pij,pjk->pik", left_imag, right_imag, precision=highest
    )
    out_imag = jnp.einsum("pij,pjk->pik", left_real, right_imag, precision=highest) + jnp.einsum(
        "pij,pjk->pik", left_imag, right_real, precision=highest
    )
    return (out_real, out_imag)


def combine_forward(earlier, later):
    return complex_product(later, earlier)


def combine_backward(earlier, later):
    return complex_product(earlier, later)


def apply_matrix(matrix, fields_now):
    mat_real, mat_imag = matrix
    vec_real = fields_now[:, 0]
    vec_imag = fields_now[:, 1]
    out_real = jnp.einsum("pij,pjk->pik", mat_real, vec_real, precision=highest) - jnp.einsum(
        "pij,pjk->pik", mat_imag, vec_imag, precision=highest
    )
    out_imag = jnp.einsum("pij,pjk->pik", mat_real, vec_imag, precision=highest) + jnp.einsum(
        "pij,pjk->pik", mat_imag, vec_real, precision=highest
    )
    return jnp.stack([out_real, out_imag], axis=1)


def apply_adjoint(matrix, fields_now):
    mat_real, mat_imag = matrix
    vec_real = fields_now[:, 0]
    vec_imag = fields_now[:, 1]
    out_real = jnp.einsum("pji,pjk->pik", mat_real, vec_real, precision=highest) + jnp.einsum(
        "pji,pjk->pik", mat_imag, vec_imag, precision=highest
    )
    out_imag = jnp.einsum("pji,pjk->pik", mat_real, vec_imag, precision=highest) - jnp.einsum(
        "pji,pjk->pik", mat_imag, vec_real, precision=highest
    )
    return jnp.stack([out_real, out_imag], axis=1)


def local(pattern, thickness, coupling, angles, points, incident, monitors, weights):
    harmonics = incident.shape[2]
    point_count = incident.shape[0]
    local_layers = pattern.shape[0]
    angle_rows = angles[points]
    identity_matrix = jnp.eye(harmonics, dtype=jnp.float32)
    layer_data = []
    for layer_index in range(local_layers):
        mixing_real = norm_scale * (identity_matrix + coupling[pattern[layer_index], 0])
        mixing_imag = norm_scale * coupling[pattern[layer_index], 1]
        phase = angle_rows * thickness[layer_index]
        cosine = jnp.cos(phase)[:, :, None]
        sine_part = jnp.sin(phase)[:, :, None]
        layer_real = cosine * mixing_real[None] - sine_part * mixing_imag[None]
        layer_imag = cosine * mixing_imag[None] + sine_part * mixing_real[None]
        layer_data.append(((layer_real, layer_imag), cosine, sine_part, mixing_real, mixing_imag))
    section = layer_data[0][0]
    layer_index = 1
    section = complex_product(layer_data[layer_index][0], section)
    section_real, section_imag = section
    eye_batch = identity_matrix[None]
    zero_batch = jnp.zeros(section_real.shape, jnp.float32)
    prefix = entering(
        (section_real, section_imag), "sect", combine_forward, (eye_batch, zero_batch), False
    )
    suffix = entering(
        (section_real, section_imag), "sect", combine_backward, (eye_batch, zero_batch), True
    )
    current = apply_matrix(prefix, incident)
    field_list = []
    for layer_index in range(local_layers):
        current = apply_matrix(layer_data[layer_index][0], current)
        field_list.append(current)
    fields = jnp.stack(field_list, axis=0)
    last_field = spread(current, "sect", lax.axis_size("sect") - 1)
    selector = jnp.sum(
        jnp.where(monitors[:, None] == jnp.arange(harmonics)[None, :], weights[:, None], 0.0),
        axis=0,
    )
    adjoint = apply_adjoint(
        suffix, last_field * selector[None, None, :, None] / (point_count * harmonics)
    )
    grad_list = []
    for layer_index in range(local_layers - 1, -1, -1):
        unused_matrix, cosine, sine_part, mixing_real, mixing_imag = layer_data[layer_index]
        layer_field = field_list[layer_index]
        adj_real = adjoint[:, 0]
        adj_imag = adjoint[:, 1]
        grad_list.append(
            -2.0
            * jnp.sum(
                angle_rows[:, :, None]
                * (adj_real * layer_field[:, 1] - adj_imag * layer_field[:, 0])
            )
        )
        back_real = cosine * adj_real + sine_part * adj_imag
        back_imag = cosine * adj_imag - sine_part * adj_real
        new_real = jnp.einsum(
            "ji,pjk->pik", mixing_real, back_real, precision=highest
        ) + jnp.einsum("ji,pjk->pik", mixing_imag, back_imag, precision=highest)
        new_imag = jnp.einsum(
            "ji,pjk->pik", mixing_real, back_imag, precision=highest
        ) - jnp.einsum("ji,pjk->pik", mixing_imag, back_real, precision=highest)
        adjoint = jnp.stack([new_real, new_imag], axis=1)
    gradient = jnp.stack(grad_list[::-1], axis=0)[None, :]
    return (fields, gradient)


def solution(mesh):
    in_specs = (
        P("sect"),
        P("sect"),
        P(),
        P(),
        P("groups"),
        P("groups", None, None, None),
        P(),
        P(),
    )
    out_specs = (P("sect", "groups", None, None, None), P("groups", "sect"))
    return jax.shard_map(local, mesh=mesh, in_specs=in_specs, out_specs=out_specs, check_vma=False)
```

profile of v0, /device:TPU:0, one launch (start us, length us, event | category | flops | bytes accessed | tf_op | source)
XLA Modules:
  0.0 395.3 jit_solution(12122222718518575283)
XLA Ops:
  15.8 1.9 constant_dynamic-slice_fusion.1
  21.6 44.9 %all-gather.9.cloned.1.call-done = f32[16,169,169]{2,1,0:T(8,128)} async-done(((f32[1,169,169]{2,1,0:T(8,128)}), f32[16,169,169]{2,1,0:T(8,128)}) %all-gather.9.cloned.1.call-update) | async-done | bytes 1827920 | tf_op jit(solution)/shard_map/all_gather | solution.py:12
  66.5 45.6 %all-gather.7.cloned.1.call-done = f32[16,169,169]{2,1,0:T(8,128)} async-done(((f32[1,169,169]{2,1,0:T(8,128)}), f32[16,169,169]{2,1,0:T(8,128)}) %all-gather.7.cloned.1.call-update) | async-done | bytes 1827920 | tf_op jit(solution)/shard_map/all_gather | solution.py:12
  112.0 81.1 %while.35 = (s32[]{:T(128)}, f32[1,169,169]{2,1,0:T(8,128)S(1)}, f32[1,169,169]{2,1,0:T(8,128)S(1)}, s32[]{:T(128)}, f32[16,1,169,169]{3,2,1,0:T(8,128)}, /*index=5*/f32[16,1,169,169]{3,2,1,0:T(8,128)}, s32[]{:T(128)}, s32[]{:T(128)}) while((s32[]{:T(128)}, f32[1,169,169]{2,1,0:T(8,128)S(1)}, f32[1,169,169]{2,1,0:T(8,128)S(1)}, ...), condition=%wide.region_1.2_spmd.clone, body=%wide.region_0.1_spmd.clone.sunk | while | flops 231886752 | bytes 2320444 | solution.py:25
  193.1 95.1 %while.36 = (s32[]{:T(128)}, f32[1,169,169]{1,2,0:T(8,128)S(1)}, f32[1,169,169]{1,2,0:T(8,128)S(1)}, s32[]{:T(128)}, f32[16,1,169,169]{3,2,1,0:T(8,128)}, /*inde...) while((s32[]{:T(128)}, f32[1,169,169]{1,2,0:T(8,128)S(1)}, ...), condition=%wide.region_3.4_spmd.clone, body=%wide.region_2.3_spmd.clone.sunk | while | flops 231886752 | bytes 2520487 | solution.py:25
  193.2 1.5 fusion.196
  194.7 1.5 fusion.194
  196.1 1.5 fusion.195
  197.6 1.5 fusion.197
  202.1 1.5 fusion.195
  203.6 1.5 fusion.197
  208.0 1.5 fusion.195
  209.5 1.5 fusion.197
  214.0 1.5 fusion.195
  215.5 1.5 fusion.197
  218.4 1.5 fusion.194
  219.9 1.5 fusion.195
  221.4 1.5 fusion.197
  222.9 1.5 fusion.196
  224.4 1.5 fusion.194
  225.8 1.5 fusion.195
  227.3 1.5 fusion.197
  228.9 1.5 fusion.196
  230.3 1.5 fusion.194
  231.8 1.5 fusion.195
  233.3 1.5 fusion.197
  234.8 1.5 fusion.196
  237.7 1.5 fusion.195
  239.2 1.5 fusion.197
  243.7 1.5 fusion.195
  245.2 1.5 fusion.197
  249.6 1.5 fusion.195
  251.1 1.5 fusion.197
  254.1 1.5 fusion.194
  255.6 1.5 fusion.195
  257.1 1.5 fusion.197
  258.6 1.5 fusion.196
  261.5 1.5 fusion.195
  263.0 1.5 fusion.197
  267.5 1.5 fusion.195
  269.0 1.5 fusion.197
  273.4 1.5 fusion.195
  274.9 1.5 fusion.197
  279.4 1.5 fusion.195
  280.8 1.5 fusion.197
  285.3 1.5 fusion.195
  286.8 1.5 fusion.197
  294.8 86.2 %all-reduce.2.cloned.1.call-done = f32[1,2,169,169]{3,2,1,0:T(8,128)} async-done(((f32[1,2,169,169]{3,2,1,0:T(8,128)}), f32[1,2,169,169]{3,2,1,0:T(8,128)}) %all-reduce.2.cloned.1.call-update) | async-done | bytes 228504 | tf_op jit(solution)/shard_map/psum | solution.py:30
  (172 shorter events, 133.0 us)
Async XLA Ops:
  7.2 6.0 %copy-start = (f32[64,169]{1,0:T(8,128)S(1)}, f32[64,169]{1,0:T(8,128)}, u32[]{:S(2)}) copy-start(f32[64,169]{1,0:T(8,128)} %param.15) | copy-start | bytes 129796
  7.2 59.3 %all-gather.9.cloned.1.call-start = ((), (), s32[]{:S(2)}) async-start(), calls=%async_computation.2 | async-start | bytes 3063808 | tf_op jit(solution)/shard_map/all_gather | solution.py:12
  15.7 5.5 %copy-start.2 = (f32[16]{0:T(128)S(1)}, f32[16]{0:T(128)}, u32[]{:S(2)}) copy-start(f32[16]{0:T(128)} %param.19) | copy-start | bytes 196
  15.8 5.5 %copy-start.3 = (s32[16]{0:T(128)S(1)}, s32[16]{0:T(128)}, u32[]{:S(2)}) copy-start(s32[16]{0:T(128)} %param.18) | copy-start | bytes 196
  15.8 5.5 %copy-start.1 = (f32[1,2,169,169]{3,1,2,0:T(2,128)S(1)}, f32[1,2,169,169]{3,1,2,0:T(2,128)}, u32[]{:S(2)}) copy-start(f32[1,2,169,169]{3,1,2,0:T(2,128)} %param.17) | copy-start | bytes 685468
  19.2 92.8 %all-gather.7.cloned.1.call-start = ((), (), s32[]{:S(2)}) async-start(), calls=%async_computation.1 | async-start | bytes 3063808 | tf_op jit(solution)/shard_map/all_gather | solution.py:12
  20.8 360.1 %all-reduce.2.cloned.1.call-start = ((), (), s32[]{:S(2)}) async-start(), calls=%async_computation | async-start | bytes 720896 | tf_op jit(solution)/shard_map/psum | solution.py:30
Sparse Core Ops, SparseCore 0:
  19.4 47.0 all-gather.8
  69.3 42.6 all-gather.6
  293.4 87.4 all-reduce.1
where the time goes:
time: 399 us; the launch traced here: 395 us
  matrix products  186 us (47%)
  waiting for transfers between devices  177 us (44%)
  between operations  19.9 us (5%)
  local copies, waits for them, and re-layouts  6.83 us (2%)
    all_gather x2, waiting for transfers between devices, entering(): everything = jax.tree.map(lambda part: lax.all_gather(part, axis), shard)  90.4 us
    psum x1, waiting for transfers between devices, spread(): return lax.psum(block, axis)  86.2 us
    dot_general x33, matrix products, complex_product(): jnp.einsum('pij,pjk->pik', left_imag, right_imag, precision=highest)  45.8 us
    dot_general x33, matrix products, complex_product(): jnp.einsum('pij,pjk->pik', left_imag, right_real, precision=highest)  44.1 us
    dot_general x33, matrix products, complex_product(): jnp.einsum('pij,pjk->pik', left_real, right_imag, precision=highest)  43.4 us
    dot_general x33, matrix products, complex_product(): jnp.einsum('pij,pjk->pik', left_real, right_real, precision=highest)  43.4 us
  transfers between devices with their start and end apart: 3, of which 3 were waited for; matrix products, arithmetic and copies ran while one was open for 1% of the time, Pallas kernels for 0%

commit v1 on v0

--- a/solution.py
+++ b/solution.py
@@ -27,7 +27,7 @@
 
 def spread(block, axis, source):
     block = jnp.where(lax.axis_index(axis) == source, block, jnp.zeros_like(block))
-    return lax.psum(block, axis)
+    return jnp.sum(lax.all_gather(block, axis), axis=0)
 
 
 def complex_product(left, right):

time: 399 us -> 317 us (0.79)
  waiting for transfers between devices: 177 us -> 90.7 us
    psum x1 -> x0, waiting for transfers between devices: 86.2 us -> none  [spread(): return lax.psum(block, axis)]
    reduce_sum x0 -> x1, other arithmetic: none -> 4.64 us  [spread(): return jnp.sum(lax.all_gather(block, axis), axis=0)]
  transfers between devices with their start and end apart: 3 -> 3, of which waited for: 3 -> 2; matrix products, arithmetic and copies ran while one was open for 1% -> 31% of each run, Pallas kernels for 0% -> 0%
where the time goes in v1:
time: 317 us; the launch traced here: 314 us
  matrix products  186 us (59%)
  waiting for transfers between devices  90.7 us (29%)
  between operations  19.9 us (6%)
  local copies, waits for them, and re-layouts  8.09 us (3%)
  other arithmetic  7.04 us (2%)
    all_gather x2, waiting for transfers between devices, entering(): everything = jax.tree.map(lambda part: lax.all_gather(part, axis), shard)  90.6 us
    dot_general x33, matrix products, complex_product(): jnp.einsum('pij,pjk->pik', left_imag, right_imag, precision=highest)  45.8 us
    dot_general x33, matrix products, complex_product(): jnp.einsum('pij,pjk->pik', left_imag, right_real, precision=highest)  44.2 us
    dot_general x33, matrix products, complex_product(): jnp.einsum('pij,pjk->pik', left_real, right_imag, precision=highest)  43.5 us
    dot_general x33, matrix products, complex_product(): jnp.einsum('pij,pjk->pik', left_real, right_real, precision=highest)  43.4 us
  transfers between devices with their start and end apart: 3, of which 2 were waited for; matrix products, arithmetic and copies ran while one was open for 31% of the time, Pallas kernels for 0%

profile of v1, /device:TPU:0, one launch (start us, length us, event | category | flops | bytes accessed | tf_op | source)
XLA Modules:
  0.0 313.9 jit_solution(4027525530323073326)
XLA Ops:
  15.8 1.9 constant_dynamic-slice_fusion.1
  21.4 45.0 %all-gather.12.cloned.1.call-done = f32[16,169,169]{2,1,0:T(8,128)} async-done(((f32[1,169,169]{2,1,0:T(8,128)}), f32[16,169,169]{2,1,0:T(8,128)}) %all-gather.12.cloned.1.call-update) | async-done | bytes 1827920 | tf_op jit(solution)/shard_map/all_gather | solution.py:12
  66.5 45.6 %all-gather.10.cloned.1.call-done = f32[16,169,169]{2,1,0:T(8,128)} async-done(((f32[1,169,169]{2,1,0:T(8,128)}), f32[16,169,169]{2,1,0:T(8,128)}) %all-gather.10.cloned.1.call-update) | async-done | bytes 1827920 | tf_op jit(solution)/shard_map/all_gather | solution.py:12
  112.0 81.1 %while.35 = (s32[]{:T(128)}, f32[1,169,169]{2,1,0:T(8,128)S(1)}, f32[1,169,169]{2,1,0:T(8,128)S(1)}, s32[]{:T(128)}, f32[16,1,169,169]{3,2,1,0:T(8,128)}, /*index=5*/f32[16,1,169,169]{3,2,1,0:T(8,128)}, s32[]{:T(128)}, s32[]{:T(128)}) while((s32[]{:T(128)}, f32[1,169,169]{2,1,0:T(8,128)S(1)}, f32[1,169,169]{2,1,0:T(8,128)S(1)}, ...), condition=%wide.region_1.2_spmd.clone, body=%wide.region_0.1_spmd.clone.sunk | while | flops 231886752 | bytes 2320444 | solution.py:25
  198.4 95.5 %while.36 = (s32[]{:T(128)}, f32[1,169,169]{1,2,0:T(8,128)S(1)}, f32[1,169,169]{1,2,0:T(8,128)S(1)}, s32[]{:T(128)}, f32[16,1,169,169]{3,2,1,0:T(8,128)}, /*inde...) while((s32[]{:T(128)}, f32[1,169,169]{1,2,0:T(8,128)S(1)}, ...), condition=%wide.region_3.4_spmd.clone, body=%wide.region_2.3_spmd.clone.sunk | while | flops 231886752 | bytes 2520487 | solution.py:25
  201.3 1.5 fusion.203
  202.8 1.5 fusion.205
  204.4 1.5 fusion.204
  207.3 1.5 fusion.203
  208.8 1.5 fusion.205
  210.3 1.5 fusion.204
  211.8 1.5 fusion.202
  213.3 1.5 fusion.203
  214.8 1.5 fusion.205
  216.3 1.5 fusion.204
  217.8 1.5 fusion.202
  219.2 1.5 fusion.203
  220.7 1.5 fusion.205
  222.3 1.5 fusion.204
  223.7 1.5 fusion.202
  225.2 1.5 fusion.203
  226.7 1.5 fusion.205
  228.2 1.5 fusion.204
  229.7 1.5 fusion.202
  231.2 1.5 fusion.203
  232.7 1.5 fusion.205
  235.7 1.5 fusion.202
  237.1 1.5 fusion.203
  238.6 1.5 fusion.205
  243.1 1.5 fusion.203
  244.6 1.5 fusion.205
  249.0 1.5 fusion.203
  250.6 1.5 fusion.205
  255.0 1.5 fusion.203
  256.5 1.5 fusion.205
  261.0 1.5 fusion.203
  262.5 1.5 fusion.205
  266.9 1.5 fusion.203
  268.4 1.5 fusion.205
  272.9 1.5 fusion.203
  274.4 1.5 fusion.205
  278.8 1.5 fusion.203
  280.3 1.5 fusion.205
  284.8 1.5 fusion.203
  286.3 1.5 fusion.205
  290.7 1.5 fusion.203
  292.2 1.5 fusion.205
  295.4 4.6 %reduce_sum.38 = f32[2,169,169]{2,0,1:T(2,128)S(1)} reduce(f32[16,1,2,169,169]{4,2,3,1,0:T(2,128)} %all-gather.8.cloned.1.call-done, f32[]{:T(128)} %constant.86.clone.1), dimensions={0,1}, to_apply=%region_4.5 | reduce | flops 856830 | bytes 3884300 | tf_op jit(solution)/shard_map/reduce_sum | solution.py:30
  (176 shorter events, 132.6 us)
Async XLA Ops:
  7.2 6.0 %copy-start = (f32[64,169]{1,0:T(8,128)S(1)}, f32[64,169]{1,0:T(8,128)}, u32[]{:S(2)}) copy-start(f32[64,169]{1,0:T(8,128)} %param.15) | copy-start | bytes 129796
  7.2 59.3 %all-gather.12.cloned.1.call-start = ((), (), s32[]{:S(2)}) async-start(), calls=%async_computation.2 | async-start | bytes 3063808 | tf_op jit(solution)/shard_map/all_gather | solution.py:12
  15.7 5.3 %copy-start.2 = (f32[16]{0:T(128)S(1)}, f32[16]{0:T(128)}, u32[]{:S(2)}) copy-start(f32[16]{0:T(128)} %param.19) | copy-start | bytes 196
  15.8 5.3 %copy-start.3 = (s32[16]{0:T(128)S(1)}, s32[16]{0:T(128)}, u32[]{:S(2)}) copy-start(s32[16]{0:T(128)} %param.18) | copy-start | bytes 196
  15.8 5.4 %copy-start.1 = (f32[1,2,169,169]{3,1,2,0:T(2,128)S(1)}, f32[1,2,169,169]{3,1,2,0:T(2,128)}, u32[]{:S(2)}) copy-start(f32[1,2,169,169]{3,1,2,0:T(2,128)} %param.17) | copy-start | bytes 685468
  19.2 92.8 %all-gather.10.cloned.1.call-start = ((), (), s32[]{:S(2)}) async-start(), calls=%async_computation.1 | async-start | bytes 3063808 | tf_op jit(solution)/shard_map/all_gather | solution.py:12
  20.8 274.6 %all-gather.8.cloned.1.call-start = ((), (), s32[]{:S(2)}) async-start(), calls=%async_computation | async-start | bytes 5883904 | tf_op jit(solution)/shard_map/all_gather | solution.py:30
Sparse Core Ops, SparseCore 0:
  19.4 47.0 all-gather.11
  69.3 42.6 all-gather.9
  198.5 55.9 all-gather.7
